TPU v7x, 32 devices: a whole 2x2x4 slice. The times are simulated.
32 devices in a mesh: bond: 8 (over z, x), mpo: 4 (over y, core).
Axes of the slice: x: 2, y: 2, z: 4, core: 2. Of those that a mesh axis runs over, the one named last changes fastest.
Arguments:
- wave_blocks: bfloat16 [8, 16, 256, 256], P('bond'), may hold values from -6 to 6
- left_environment: bfloat16 [8, 8, 256, 256], P('mpo', 'bond'), may hold values from -0.375 to 0.375
- right_environment: bfloat16 [8, 8, 256, 256], P('mpo', 'bond'), may hold values from -0.375 to 0.375
- site_operators: bfloat16 [8, 16, 16], P('mpo'), may hold values from -1.1953125 to 1.1953125
- right_sector: int32 [8, 16, 1], P('bond'), may hold values from 0 to 7; in each aligned block of 16 rows (0 to 15, 16 to 31, ..., all dimensions but the last counted through in order) at most 2 rows name the same one
- left_sizes: int32 [8], replicated, may hold values from 128 to 256
- right_sizes: int32 [8], replicated, may hold values from 128 to 256
- sector_place: int32 [8], replicated, may hold values from 0 to 7, each once
Outputs:
- applied: bfloat16 [8, 16, 256, 256], P('bond', 'mpo')
Inputs may be any that keep to these rules, and one draw needn't show every extreme that they name: `right_sector`: among the 16 blocks of one bond index no right sector is named more than 2 times, a bound that some block reaches. `sector_place`: every position is taken by exactly one right sector.
All inputs are finite; a program needn't handle non-finite values.
Results may differ from a plain program's by a relative error of at most 0.0057.
Values may be sent and summed in bfloat16 or wider, within the bound.
A program may use at most 64 MiB of HBM per device.

v0:
```python
import jax
import jax.numpy as jnp
from jax import lax
from jax.sharding import PartitionSpec as P


def lookup(entries, indices):
    count = entries.shape[0]
    matches = indices[..., None] == jnp.arange(count, dtype=jnp.int32)
    return jnp.sum(jnp.where(matches, entries, 0), axis=-1)


def shards(
    wave_blocks,
    left_environment,
    right_environment,
    site_operators,
    right_sector,
    left_sizes,
    right_sizes,
    sector_place,
):
    sectors = wave_blocks.shape[0]
    states = wave_blocks.shape[1]
    block_rows = wave_blocks.shape[2]
    channels = left_environment.shape[0]
    first_sector = lax.axis_index("bond") * sectors
    sector_ids = right_sector[:, :, 0]
    offsets = jnp.arange(block_rows, dtype=jnp.int32)
    left_live = lax.dynamic_slice_in_dim(left_sizes, first_sector, sectors)
    row_mask = offsets[None, :] < left_live[:, None]
    column_mask = offsets[None, None, :] < lookup(right_sizes, sector_ids)[:, :, None]
    live_mask = row_mask[:, None, :, None] & column_mask[:, :, None, :]
    masked = jnp.where(live_mask, wave_blocks, jnp.zeros((), jnp.bfloat16))
    block_count = sectors * states
    flat_blocks = masked.reshape(block_count, block_rows, block_rows)
    place_flat = lookup(sector_place, sector_ids).reshape(block_count)
    gathered = lax.all_gather(right_environment, "bond", axis=1, tiled=True)
    chosen = jnp.take(gathered, place_flat, axis=1)
    right_part = jnp.einsum(
        "bac,hbxc->bhax", flat_blocks, chosen, preferred_element_type=jnp.float32
    ).astype(jnp.bfloat16)
    right_part = right_part.reshape(sectors, states, channels, block_rows, block_rows)
    same_sector = sector_ids[:, :, None] == sector_ids[:, None, :]
    mixing = jnp.where(same_sector[:, None], site_operators[None], jnp.zeros((), jnp.bfloat16))
    mixed = jnp.einsum(
        "nhst,nthac->nshac", mixing, right_part, preferred_element_type=jnp.float32
    ).astype(jnp.bfloat16)
    partial_value = jnp.einsum(
        "hnab,nshbc->nsac", left_environment, mixed, preferred_element_type=jnp.float32
    )
    per_device = states // lax.axis_size("mpo")
    first_state = lax.axis_index("mpo") * per_device
    summed = lax.psum(partial_value, "mpo")
    summed = lax.dynamic_slice_in_dim(summed, first_state, per_device, 1)
    kept_mask = lax.dynamic_slice_in_dim(live_mask, first_state, per_device, 1)
    return jnp.where(kept_mask, summed, jnp.zeros((), jnp.float32)).astype(jnp.bfloat16)


def solution(mesh):
    placed = (
        P("bond", None, None, None),
        P("mpo", "bond", None, None),
        P("mpo", "bond", None, None),
        P("mpo", None, None),
        P("bond", None, None),
        P(),
        P(),
        P(),
    )
    return jax.shard_map(
        shards, mesh=mesh, in_specs=placed, out_specs=P("bond", "mpo", None, None), check_vma=False
    )
```

profile of v0, /device:TPU:0, one launch (start us, length us, event | category | flops | bytes accessed | tf_op | source)
XLA Modules:
  0.0 172.7 jit_solution(5104987714782508854)
XLA Ops:
  6.5 0.0 copy-start
  6.5 0.0 copy-start.5
  6.5 0.0 copy-start.2
  6.5 0.0 copy-start.3
  6.5 0.0 copy-start.4
  6.5 0.0 all-gather.2.cloned.1.call-start
  6.6 0.7 all-gather.2.cloned.1.call-update
  7.3 2.9 %copy.12 = bf16[1,16,256,256]{2,3,1,0:T(8,128)(2,1)S(1)} copy(bf16[1,16,256,256]{3,2,1,0:T(8,128)(2,1)} %param.8) | data formatting | bytes 4194304 | tf_op args[0]
  10.2 0.0 copy-done.5
  10.2 0.6 dynamic_slice.9
  10.8 0.6 iota_compare_fusion.2
  11.4 0.0 copy-done.2
  11.4 0.0 copy-done.3
  11.4 0.0 copy-done.4
  11.4 0.1 select_reduce_fusion.1
  11.6 0.1 broadcast_compare_fusion
  11.6 0.1 iota_compare_fusion
  11.7 2.0 %broadcast_and_fusion = pred[1,16,256,256]{2,3,1,0:T(8,128)(4,1)} fusion(pred[16,256]{1,0:T(8,128)(4,1)S(1)} %iota_compare_fusion, pred[256]{0:T(512)(128)(4,1)S(1)} %iota_compare_fusion.2), kind=kLoop, calls=%fused_computation.15 | loop fusion | flops 1048576 | bytes 1052928 | tf_op jit(solution)/shard_map/and | solution.py:33
  13.7 47.6 %all-gather.2.cloned.1.call-done = bf16[2,8,256,256]{3,2,1,0:T(8,128)(2,1)} async-done(((bf16[2,1,256,256]{3,2,1,0:T(8,128)(2,1)}), bf16[2,8,256,256]{3,2,1,0:T(8,128)(2,1)}) %all-gather.2.cloned.1.call-update) | async-done | bytes 2097168 | tf_op jit(solution)/shard_map/all_gather | solution.py:38
  61.4 4.3 %gather_fusion = bf16[16,2,256,256]{3,2,1,0:T(8,128)(2,1)} fusion(bf16[2,8,256,256]{3,2,1,0:T(8,128)(2,1)} %all-gather.2.cloned.1.call-done, s32[1024]{0:T(1024)S(1)} %pad_clamp_fusion), kind=kCustom, calls=%fused_computation | custom fusion | bytes 8388672 | tf_op jit(solution)/shard_map/jit(_take)/gather | solution.py:39
  65.7 4.7 %fusion.2 = bf16[16,2,256,256]{3,2,1,0:T(8,128)(2,1)} fusion(bf16[16,2,256,256]{3,2,1,0:T(8,128)(2,1)} %gather_fusion, pred[16]{0:T(512)(128)(4,1)S(1)} %compare_and_fusion, bf16[1,16,256,256]{2,3,1,0:T(8,128)(2,1)S(1)} %copy.12, pred[16,256]{1,0:T(8,128)(4,1)S(1)} %iota_compare_fusion, pred[256]{0:T(512)(128)(4,1)S(1)} %iota_compare_fusion.2), kind=kOutput, calls=%fused_computation.3 | convolution fusion | flops 1077936128 | bytes 10490128 | tf_op jit(solution)/shard_map/bac,hbxc->bhax/dot_general | solution.py:40
  70.4 0.0 copy-start.1
  70.4 7.9 %copy.16 = bf16[16,2,256,256]{2,0,3,1:T(8,128)(2,1)} copy(bf16[16,2,256,256]{3,2,1,0:T(8,128)(2,1)} %fusion.2) | data formatting | bytes 8388608 | tf_op jit(solution)/shard_map/bac,hbxc->bhax/dot_general | solution.py:40
  78.3 0.0 copy-done.1
  78.3 3.4 %convert_bitcast_fusion = bf16[16,2,256,256]{3,0,2,1:T(8,128)(2,1)S(1)} fusion(bf16[16,2,256,256]{2,0,3,1:T(8,128)(2,1)} %copy.16, bf16[2,16,16]{2,1,0:T(8,128)(2,1)S(1)} %copy-done.1, pred[16,16]{1,0:T(8,128)(4,1)S(1)} %broadcast_compare_fusion), kind=kOutput, calls=%fused_computation.8 | convolution fusion | flops 69206528 | bytes 8389888 | tf_op jit(solution)/shard_map/nhst,nthac->nshac/dot_general | solution.py:46
  81.7 0.0 copy-done
  81.7 6.1 %fusion.11 = f32[1,16,256,256]{2,3,1,0:T(8,128)} fusion(bf16[16,2,256,256]{3,0,2,1:T(8,128)(2,1)S(1)} %convert_bitcast_fusion, bf16[2,1,256,256]{3,2,1,0:T(8,128)(2,1)S(1)} %copy-done), kind=kOutput, calls=%fused_computation.11 | convolution fusion | flops 1073741824 | bytes 8650752 | tf_op jit(solution)/shard_map/hnab,nshbc->nsac/dot_general | solution.py:49
  87.8 75.9 %all-reduce.1 = bf16[1,16,256,256]{2,3,1,0:T(8,128)(2,1)S(1)} all-reduce(f32[1,16,256,256]{2,3,1,0:T(8,128)} %fusion.11), channel_id=1, replica_groups=mesh['bond'=8,'mpo'=4] {'mpo'}, use_global_device_ids=true, to_apply=%region_2.3 | all-reduce | flops 1048576 | bytes 6291456 | tf_op jit(solution)/shard_map/psum | solution.py:54
  163.7 1.1 select_convert_fusion
  164.8 1.0 copy.14
  (3 shorter events, 0.0 us)
Async XLA Ops:
  6.5 75.1 %copy-start = (bf16[2,1,256,256]{3,2,1,0:T(8,128)(2,1)S(1)}, bf16[2,1,256,256]{3,2,1,0:T(8,128)(2,1)}, u32[]{:S(2)}) copy-start(bf16[2,1,256,256]{3,2,1,0:T(8,128)(2,1)} %param.9) | copy-start | bytes 786436
  6.5 3.6 %copy-start.5 = (s32[8]{0:T(128)S(1)}, s32[8]{0:T(128)}, u32[]{:S(2)}) copy-start(s32[8]{0:T(128)} %param.13) | copy-start | bytes 100
  6.5 4.9 %copy-start.2 = (s32[1,16,1]{1,2,0:T(1,128)S(1)}, s32[1,16,1]{1,2,0:T(1,128)}, u32[]{:S(2)}) copy-start(s32[1,16,1]{1,2,0:T(1,128)} %param.12) | copy-start | bytes 196
  6.5 4.9 %copy-start.3 = (s32[8]{0:T(128)S(1)}, s32[8]{0:T(128)}, u32[]{:S(2)}) copy-start(s32[8]{0:T(128)} %param.14) | copy-start | bytes 100
  6.5 4.9 %copy-start.4 = (s32[8]{0:T(128)S(1)}, s32[8]{0:T(128)}, u32[]{:S(2)}) copy-start(s32[8]{0:T(128)} %param.15) | copy-start | bytes 100
  6.5 54.8 %all-gather.2.cloned.1.call-start = ((), (), s32[]{:S(2)}) async-start(), calls=%async_computation | async-start | bytes 2359296 | tf_op jit(solution)/shard_map/all_gather | solution.py:38
  70.4 7.9 %copy-start.1 = (bf16[2,16,16]{2,1,0:T(8,128)(2,1)S(1)}, bf16[2,16,16]{2,1,0:T(8,128)(2,1)}, u32[]{:S(2)}) copy-start(bf16[2,16,16]{2,1,0:T(8,128)(2,1)} %param.11) | copy-start | bytes 3076
Sparse Core Ops, SparseCore 0:
  9.5 51.7 all-gather.1
where the time goes:
time: 173 us
  blocking collectives  75.9 us (44%)
  waiting for transfers between devices  48.3 us (28%)
  local copies, waits for them, and re-layouts  16.7 us (10%)
  matrix products  14.2 us (8%)
  between operations  13.5 us (8%)
  other arithmetic  4.04 us (2%)
    psum x1, blocking collectives, shards(): summed = lax.psum(partial_value, 'mpo')  75.9 us
    all_gather x1, waiting for transfers between devices, shards(): gathered = lax.all_gather(right_environment, 'bond', axis=1, tiled=True)  47.6 us
    dot_general x1, local copies, waits for them, and re-layouts, shards(): jnp.einsum('bac,hbxc->bhax', flat_blocks, chosen, preferred_element_type=...  7.89 us
    dot_general x1, matrix products, shards(): jnp.einsum('hnab,nshbc->nsac', left_environment, mixed, preferred_element...  6.13 us
    dot_general x1, matrix products, shards(): jnp.einsum('bac,hbxc->bhax', flat_blocks, chosen, preferred_element_type=...  4.66 us
    gather x1, local copies, waits for them, and re-layouts, shards(): chosen = jnp.take(gathered, place_flat, axis=1)  4.34 us
  transfers between devices with their start and end apart: 1, of which 1 were waited for; matrix products, arithmetic and copies ran while one was open for 4% of the time, Pallas kernels for 0%

commit v1 on v0

--- a/solution.py
+++ b/solution.py
@@ -51,7 +51,7 @@
     )
     per_device = states // lax.axis_size("mpo")
     first_state = lax.axis_index("mpo") * per_device
-    summed = lax.psum(partial_value, "mpo")
+    summed = jnp.sum(lax.all_gather(partial_value, "mpo"), axis=0)
     summed = lax.dynamic_slice_in_dim(summed, first_state, per_device, 1)
     kept_mask = lax.dynamic_slice_in_dim(live_mask, first_state, per_device, 1)
     return jnp.where(kept_mask, summed, jnp.zeros((), jnp.float32)).astype(jnp.bfloat16)

time: 173 us -> 214 us (1.24)
  waiting for transfers between devices: 48.3 us -> 155 us
  blocking collectives: 75.9 us -> 0 us
  other arithmetic: 4.04 us -> 11.4 us
    all_gather x0 -> x1, waiting for transfers between devices: none -> 104 us  [shards(): summed = jnp.sum(lax.all_gather(partial_value, 'mpo'), axis=0)]
    psum x1 -> x0, blocking collectives: 75.9 us -> none  [shards(): summed = lax.psum(partial_value, 'mpo')]
    dot_general x1 -> x0, local copies, waits for them, and re-layouts: 7.89 us -> none  [shards(): jnp.einsum('bac,hbxc->bhax', flat_blocks, chosen, preferred_element_type=...]
    reduce_sum x0 -> x1, other arithmetic: none -> 7.51 us  [shards(): summed = jnp.sum(lax.all_gather(partial_value, 'mpo'), axis=0)]
    convert_element_type x1, local copies, waits for them, and re-layouts: 1 us -> 7.89 us  [shards(): right_part = jnp.einsum('bac,hbxc->bhax', flat_blocks, chosen, preferred_...]
    transpose x0 -> x1, local copies, waits for them, and re-layouts: none -> 5.35 us  [shards(): jnp.einsum('hnab,nshbc->nsac', left_environment, mixed, preferred_element...]
    unnamed x13 -> x6, local copies, waits for them, and re-layouts: 2.88 us -> 0.01 us
    all_gather x1, waiting for transfers between devices: 47.6 us -> 50.4 us  [shards(): gathered = lax.all_gather(right_environment, 'bond', axis=1, tiled=True)]
  transfers between devices with their start and end apart: 1 -> 2, of which waited for: 1 -> 2; matrix products, arithmetic and copies ran while one was open for 4% -> 2% of each run, Pallas kernels for 0% -> 0%
where the time goes in v1:
time: 214 us
  waiting for transfers between devices  155 us (72%)
  local copies, waits for them, and re-layouts  18.8 us (9%)
  matrix products  15.1 us (7%)
  between operations  13.5 us (6%)
  other arithmetic  11.4 us (5%)
    all_gather x1, waiting for transfers between devices, shards(): summed = jnp.sum(lax.all_gather(partial_value, 'mpo'), axis=0)  104 us
    all_gather x1, waiting for transfers between devices, shards(): gathered = lax.all_gather(right_environment, 'bond', axis=1, tiled=True)  50.4 us
    convert_element_type x1, local copies, waits for them, and re-layouts, shards(): right_part = jnp.einsum('bac,hbxc->bhax', flat_blocks, chosen, preferred_...  7.89 us
    reduce_sum x1, other arithmetic, shards(): summed = jnp.sum(lax.all_gather(partial_value, 'mpo'), axis=0)  7.51 us
    dot_general x1, matrix products, shards(): jnp.einsum('hnab,nshbc->nsac', left_environment, mixed, preferred_element...  6.13 us
    dot_general x1, matrix products, shards(): jnp.einsum('bac,hbxc->bhax', flat_blocks, chosen, preferred_element_type=...  5.54 us
    transpose x1, local copies, waits for them, and re-layouts, shards(): jnp.einsum('hnab,nshbc->nsac', left_environment, mixed, preferred_element...  5.35 us
    gather x1, local copies, waits for them, and re-layouts, shards(): chosen = jnp.take(gathered, place_flat, axis=1)  4.34 us
  transfers between devices with their start and end apart: 2, of which 2 were waited for; matrix products, arithmetic and copies ran while one was open for 2% of the time, Pallas kernels for 0%

profile of v1, /device:TPU:0, one launch (start us, length us, event | category | flops | bytes accessed | tf_op | source)
XLA Modules:
  0.0 214.0 jit_solution(14440453127684700390)
XLA Ops:
  6.5 0.0 copy-start
  6.5 0.0 all-gather.4.cloned.1.call-start
  6.5 0.7 all-gather.4.cloned.1.call-update
  7.3 0.0 all-gather.6.cloned.1.call-start
  7.3 1.2 dynamic_slice.9
  8.6 0.6 iota_compare_fusion.2
  9.2 0.8 select_reduce_fusion.1
  10.0 0.8 broadcast_compare_fusion
  10.8 0.1 iota_compare_fusion
  10.9 0.0 copy-start.2
  10.9 50.4 %all-gather.4.cloned.1.call-done = bf16[2,8,256,256]{3,2,1,0:T(8,128)(2,1)} async-done(((bf16[2,1,256,256]{3,2,1,0:T(8,128)(2,1)}), bf16[2,8,256,256]{3,2,1,0:T(8,128)(2,1)}) %all-gather.4.cloned.1.call-update) | async-done | bytes 2097168 | tf_op jit(solution)/shard_map/all_gather | solution.py:38
  61.3 4.3 %gather_fusion = bf16[16,2,256,256]{3,2,1,0:T(8,128)(2,1)} fusion(bf16[2,8,256,256]{3,2,1,0:T(8,128)(2,1)} %all-gather.4.cloned.1.call-done, s32[1024]{0:T(1024)S(1)} %pad_clamp_fusion), kind=kCustom, calls=%fused_computation | custom fusion | bytes 8388672 | tf_op jit(solution)/shard_map/jit(_take)/gather | solution.py:39
  65.7 0.0 copy-done.2
  65.7 5.5 %convert_bitcast_fusion.1 = bf16[16,2,256,256]{2,3,1,0:T(8,128)(2,1)} fusion(bf16[16,2,256,256]{3,2,1,0:T(8,128)(2,1)} %gather_fusion, pred[16]{0:T(512)(128)(4,1)S(1)} %compare_and_fusion, bf16[1,16,256,256]{3,2,1,0:T(8,128)(2,1)S(1)} %copy-done.2, pred[16,256]{1,0:T(8,128)(4,1)S(1)} %iota_compare_fusion, pred[256]{0:T(512)(128)(4,1)S(1)} %iota_compare_fusion.2), kind=kOutput, calls=%fused_computation.7 | convolution fusion | flops 1080033280 | bytes 10490128 | tf_op jit(solution)/shard_map/bac,hbxc->bhax/dot_general | solution.py:40
  71.2 0.0 copy-start.1
  71.2 7.9 %copy.18 = bf16[16,2,256,256]{3,0,2,1:T(8,128)(2,1)} copy(bf16[16,2,256,256]{2,3,1,0:T(8,128)(2,1)} %convert_bitcast_fusion.1) | data formatting | bytes 8388608 | tf_op jit(solution)/shard_map/convert_element_type | solution.py:42
  79.1 0.0 copy-done.1
  79.1 3.4 %convert_bitcast_fusion = bf16[16,2,256,256]{3,0,2,1:T(8,128)(2,1)S(1)} fusion(bf16[16,2,256,256]{3,0,2,1:T(8,128)(2,1)} %copy.18, bf16[2,16,16]{2,1,0:T(8,128)(2,1)S(1)} %copy-done.1, pred[16,16]{1,0:T(8,128)(4,1)S(1)} %broadcast_compare_fusion), kind=kOutput, calls=%fused_computation.6 | convolution fusion | flops 69206528 | bytes 8389888 | tf_op jit(solution)/shard_map/nhst,nthac->nshac/dot_general | solution.py:46
  82.5 0.0 copy-done
  82.5 6.1 %fusion.8 = f32[1,16,256,256]{2,3,1,0:T(8,128)} fusion(bf16[16,2,256,256]{3,0,2,1:T(8,128)(2,1)S(1)} %convert_bitcast_fusion, bf16[2,1,256,256]{3,2,1,0:T(8,128)(2,1)S(1)} %copy-done), kind=kOutput, calls=%fused_computation.9 | convolution fusion | flops 1073741824 | bytes 8650752 | tf_op jit(solution)/shard_map/hnab,nshbc->nsac/dot_general | solution.py:49
  88.7 5.3 %copy.20 = f32[1,16,256,256]{3,2,1,0:T(8,128)} copy(f32[1,16,256,256]{2,3,1,0:T(8,128)} %fusion.8) | data formatting | bytes 8388608 | tf_op jit(solution)/shard_map/hnab,nshbc->nsac/transpose | solution.py:49
  94.0 0.0 all-gather.6.cloned.1.call-update
  94.0 0.6 broadcast_and_fusion
  94.7 104.0 %all-gather.6.cloned.1.call-done = f32[4,16,256,256]{3,2,1,0:T(8,128)} async-done(((f32[1,16,256,256]{3,2,1,0:T(8,128)}), f32[4,16,256,256]{3,2,1,0:T(8,128)}) %all-gather.6.cloned.1.call-update) | async-done | bytes 16777232 | tf_op jit(solution)/shard_map/all_gather | solution.py:54
  198.6 7.5 %reduce.3 = bf16[16,256,256]{2,1,0:T(8,128)(2,1)S(1)} reduce(f32[4,16,256,256]{3,2,1,0:T(8,128)} %all-gather.6.cloned.1.call-done, f32[]{:T(128)} %constant.34.clone.1), dimensions={0}, to_apply=%region_2.3 | reduce | flops 3145728 | bytes 18874372 | tf_op jit(solution)/shard_map/reduce_sum | solution.py:54
  206.2 1.0 fusion.14
  (3 shorter events, 0.0 us)
Async XLA Ops:
  6.5 76.0 %copy-start = (bf16[2,1,256,256]{3,2,1,0:T(8,128)(2,1)S(1)}, bf16[2,1,256,256]{3,2,1,0:T(8,128)(2,1)}, u32[]{:S(2)}) copy-start(bf16[2,1,256,256]{3,2,1,0:T(8,128)(2,1)} %param.9) | copy-start | bytes 786436
  6.5 54.8 %all-gather.4.cloned.1.call-start = ((), (), s32[]{:S(2)}) async-start(), calls=%async_computation | async-start | bytes 2359296 | tf_op jit(solution)/shard_map/all_gather | solution.py:38
  7.3 191.4 %all-gather.6.cloned.1.call-start = ((), (), s32[]{:S(2)}) async-start(), calls=%async_computation.1 | async-start | bytes 20971520 | tf_op jit(solution)/shard_map/all_gather | solution.py:54
  10.9 54.8 %copy-start.2 = (bf16[1,16,256,256]{3,2,1,0:T(8,128)(2,1)S(1)}, bf16[1,16,256,256]{3,2,1,0:T(8,128)(2,1)}, u32[]{:S(2)}) copy-start(bf16[1,16,256,256]{3,2,1,0:T(8,128)(2,1)} %param.8) | copy-start | bytes 6291460
  71.2 7.9 %copy-start.1 = (bf16[2,16,16]{2,1,0:T(8,128)(2,1)S(1)}, bf16[2,16,16]{2,1,0:T(8,128)(2,1)}, u32[]{:S(2)}) copy-start(bf16[2,16,16]{2,1,0:T(8,128)(2,1)} %param.11) | copy-start | bytes 3076
Sparse Core Ops, SparseCore 0:
  9.5 51.7 all-gather.3
  94.2 104.4 all-gather.5
